TPU v7x, 32 devices: a whole 2x2x4 slice. The times are simulated.
32 devices in a mesh: segment: 4 (over y, x), lane: 8 (over z, core).
Axes of the slice: x: 2, y: 2, z: 4, core: 2. Of those that a mesh axis runs over, the one named last changes fastest.
Arguments:
- spectra: float32 [4, 4096, 1024], P(None, 'lane'), may hold values from -6 to 6
- rfi_flags: int32 [4, 4096, 8], P(None, 'lane'), may hold values 0 or 1
- sub_delay: int32 [64, 4096], P(None, 'lane'), may hold values from 0 to 7
- fine_delay: int32 [2048, 64], P('lane'), may hold values from 0 to 31
- widths: int32 [8], replicated, may hold values from 1 to 64
Outputs:
- peaks: float32 [4, 2048, 8], P('segment', 'lane')
All inputs are finite; a program needn't handle non-finite values. No bound on the sum of `rfi_flags` on one device may be relied on, other than what follows from the above.
Results may differ from a plain program's by a relative error of at most 0.0001.
Values sent between devices are 32-bit elements; how exact they have to be, the bound alone decides.
A program may use at most 128 MiB of HBM per device.

v0:
```python
import jax
import jax.numpy as jnp
from jax import lax
from jax.sharding import PartitionSpec as P

C = 4096
SUBCH = 64
NSUB = 64
NCOARSE = 64
NDM = 2048
D1 = 8
D2 = 32


delay_group = 4


def clean_block(power_in, flag_rows, block_len):
    row_count, samples = power_in.shape
    kept_mask = 1.0 - flag_rows.astype(jnp.float32)
    kept_mask = jnp.broadcast_to(
        kept_mask[:, :, None], (row_count, flag_rows.shape[1], block_len)
    ).reshape(row_count, samples)
    masked = kept_mask * power_in
    centre = jnp.mean(masked, axis=1, keepdims=True)
    spread = jnp.mean((masked - centre) * (masked - centre), axis=1, keepdims=True)
    return kept_mask * (power_in - centre) * lax.rsqrt(spread + 1e-05)


def detect(centered, widths, total_sq, cell_count):
    sigma = jnp.sqrt(total_sq / cell_count + 1e-06)
    samples = centered.shape[1]
    prefix = jnp.concatenate(
        [jnp.zeros((centered.shape[0], 1), jnp.float32), jnp.cumsum(centered, axis=1)], axis=1
    )
    sample_idx = jnp.arange(samples, dtype=jnp.int32)
    ends = jnp.minimum(sample_idx[None, :] + widths[:, None], samples)
    upper = prefix[:, ends]
    lower = prefix[:, None, :samples]
    scaled = (upper - lower) / (sigma * jnp.sqrt(widths.astype(jnp.float32)))[None, :, None]
    return jnp.max(scaled, axis=2)


def subband_sums(cleaned, sub_delay, sub_width, delays):
    row_count, samples = cleaned.shape
    groups = row_count // sub_width
    coarse = sub_delay.shape[0]
    levels = jnp.arange(delays, dtype=jnp.int32)
    onehot = (
        sub_delay.reshape(coarse, groups, 1, sub_width) == levels[None, None, :, None]
    ).astype(jnp.float32)
    weights_all = onehot.transpose(1, 0, 2, 3)
    padded = jnp.pad(cleaned.reshape(groups, sub_width, samples), ((0, 0), (0, 0), (0, delays)))
    totals = jnp.zeros((coarse, groups, samples), jnp.float32)
    for first_lag in range(0, delays, delay_group):
        span_here = min(delay_group, delays - first_lag)
        stacked = jnp.stack(
            [
                padded[:, :, first_lag + offset : first_lag + offset + samples]
                for offset in range(span_here)
            ],
            axis=1,
        )
        stacked = stacked.reshape(groups, span_here * sub_width, samples)
        weights = weights_all[:, :, first_lag : first_lag + span_here, :].reshape(
            groups, coarse, span_here * sub_width
        )
        totals = totals + jnp.einsum(
            "bkx,bxs->kbs", weights, stacked, precision=lax.Precision.HIGHEST
        )
    return (totals, jnp.sum(onehot, axis=3))


def fine_sums(source, onehot):
    groups, bands, samples = source.shape
    per_group = onehot.shape[1]
    delays = onehot.shape[2]
    padded = jnp.pad(source, ((0, 0), (0, 0), (0, delays)))
    running = jnp.zeros((groups, per_group, samples), jnp.float32)
    for first_lag in range(0, delays, delay_group):
        span_here = min(delay_group, delays - first_lag)
        stacked = jnp.stack(
            [
                padded[:, :, first_lag + offset : first_lag + offset + samples]
                for offset in range(span_here)
            ],
            axis=1,
        )
        stacked = stacked.reshape(groups, span_here * bands, samples)
        weights = onehot[:, :, first_lag : first_lag + span_here, :].reshape(
            groups, per_group, span_here * bands
        )
        running = running + jnp.einsum(
            "gjx,gxs->gjs", weights, stacked, precision=lax.Precision.HIGHEST
        )
    return running.reshape(groups * per_group, samples)


def body(spectra, rfi_flags, sub_delay, fine_delay, widths):
    lane_count = lax.axis_size("lane")
    section_count = lax.axis_size("segment")
    section_idx = lax.axis_index("segment")
    batches, row_count, samples = spectra.shape
    block_len = samples // rfi_flags.shape[2]
    coarse_dev = NCOARSE // lane_count
    dm_dev = fine_delay.shape[0]
    per_coarse = dm_dev // coarse_dev
    fine_levels = jnp.arange(D2, dtype=jnp.int32)
    fine_hot = (fine_delay[:, None, :] == fine_levels[None, :, None]).astype(jnp.float32)
    fine_hot = fine_hot.reshape(coarse_dev, per_coarse, D2, NSUB)
    per_section = batches // section_count
    batch_pos = section_idx * per_section + 0
    power_now = lax.dynamic_index_in_dim(spectra, batch_pos, 0, keepdims=False)
    flags_now = lax.dynamic_index_in_dim(rfi_flags, batch_pos, 0, keepdims=False)
    normed = clean_block(power_now, flags_now, block_len)
    channel_sum = lax.psum(jnp.sum(normed, axis=0), "lane")
    cleaned = normed - (channel_sum / C)[None, :]
    totals, counts = subband_sums(cleaned, sub_delay, SUBCH, D1)
    moved = lax.all_to_all(totals, "lane", split_axis=0, concat_axis=1, tiled=True)
    series = fine_sums(moved, fine_hot)
    centered = series - jnp.mean(series, axis=1, keepdims=True)
    total_sq = lax.psum(jnp.sum(centered * centered), "lane")
    outputs = [detect(centered, widths, total_sq, NDM * samples)]
    return jnp.stack(outputs)


def solution(mesh):
    in_specs = (P(None, "lane", None), P(None, "lane", None), P(None, "lane"), P("lane", None), P())
    out_specs = P("segment", "lane", None)
    return jax.shard_map(body, mesh=mesh, in_specs=in_specs, out_specs=out_specs, check_vma=False)
```

profile of v0, /device:TPU:0, one launch (start us, length us, event | category | flops | bytes accessed | tf_op | source)
XLA Modules:
  0.0 329.9 jit_solution(10740747146912169289)
XLA Ops:
  6.0 3.8 %fusion.43 = (f32[512]{0:T(512)S(1)}, f32[1,512,1024]{2,1,0:T(8,128)}, f32[1,512,1024]{2,1,0:T(8,128)S(1)}) fusion(f32[1,512,1024]{2,1,0:T(8,128)} %broadcast_in_dim.5, f32[4,512,1024]{2,1,0:T(8,128)} %param.5, s32[]{:T(128)S(6)} %select_n.16), kind=kLoop, calls=%fused_computation.122 | loop fusion | flops 1048064 | bytes 8390660 | tf_op jit(solution)/shard_map/reduce_sum | solution.py:25
  13.8 18.1 %psum.14 = f32[1024]{0:T(1024)S(1)} all-reduce(f32[1024]{0:T(1024)S(1)} %multiply_reduce_fusion), channel_id=1, replica_groups=mesh['segment'=4,'lane'=8] {'lane'}, use_global_device_ids=true, to_apply=%region_3.4 | all-reduce | flops 1024 | bytes 8192 | tf_op jit(solution)/shard_map/psum | solution.py:116
  33.9 5.5 %fusion.35 = (f32[8,1,64,1024]{3,2,0,1:T(8,128)S(1)}, f32[8,1,64,1024]{3,2,1,0:T(8,128)}, f32[8,1,64,1024]{3,2,1,0:T(8,128)}, f32[8,1,64,1024]{3,2,0,1:T(8,128)S...) fusion(f32[8,64,1024]{2,1,0:T(8,128)S(1)} %multiply_subtract_fusion), kind=kLoop, calls=%fused_computation.86 | loop fusion | bytes 16777216 | tf_op jit(solution)/shard_map/stack | solution.py:57
  40.5 4.1 %copy.61 = f32[8,4,64,1024]{3,2,1,0:T(8,128)} copy(f32[8,4,64,1024]{3,2,0,1:T(8,128)S(1)} %pad_maximum_fusion.1) | data formatting | bytes 16777216 | tf_op jit(solution)/shard_map/stack | solution.py:57
  48.7 3.2 pad_maximum_fusion
  51.9 3.3 %fusion.47 = f32[8,1024,64]{1,2,0:T(8,128)S(1)} fusion(f32[8,256,1024]{2,1,0:T(8,128)S(1)} %bitcast.161, pred[8,64,256]{2,1,0:T(32,128)(4,1)S(1)} %reshape.277), kind=kOutput, calls=%fused_computation.126 | convolution fusion | flops 1610612736 | bytes 10616832 | tf_op jit(solution)/shard_map/bkx,bxs->kbs/dot_general | solution.py:68
  55.3 3.4 %add_bitcast_fusion = f32[64,8,1024]{2,0,1:T(8,128)S(1)} fusion(f32[8,1024,64]{1,2,0:T(8,128)S(1)} %fusion.47, f32[8,256,1024]{2,1,0:T(8,128)S(1)} %bitcast.159, pred[8,64,256]{2,1,0:T(32,128)(4,1)S(1)} %reshape.279), kind=kOutput, calls=%fused_computation.90 | convolution fusion | flops 1611137024 | bytes 12713984 | tf_op jit(solution)/shard_map/bkx,bxs->kbs/dot_general | solution.py:68
  61.2 4.1 %all-to-all-start = ((f32[64,8,1024]{2,1,0:T(8,128)}), f32[64,8,1024]{2,1,0:T(8,128)S(1)}, u32[]{:S(2)}, u32[]{:S(2)}) async-start(f32[64,8,1024]{2,1,0:T(8,128)} %copy.62), calls=%async_computation | async-start | bytes 4194304 | tf_op jit(solution)/shard_map/all_to_all | solution.py:119
  69.2 45.1 %all-to-all-done = f32[64,8,1024]{2,1,0:T(8,128)S(1)} async-done(((f32[64,8,1024]{2,1,0:T(8,128)}), f32[64,8,1024]{2,1,0:T(8,128)S(1)}, u32[]{:S(2)}, u32[]{:S(2)}) %all-to-all-start) | async-done | bytes 2097184 | tf_op jit(solution)/shard_map/all_to_all | solution.py:119
  114.6 11.6 %fusion.29 = (f32[8,1,64,1024]{3,2,0,1:T(8,128)}, f32[8,1,64,1024]{3,2,0,1:T(8,128)}, f32[8,1,64,1024]{3,2,0,1:T(8,128)}, f32[8,1,64,1024]{3,2,0,1:T(8,128)}, f3...) fusion(f32[8,64,1024]{2,1,0:T(8,128)S(1)} %bitcast.162), kind=kLoop, calls=%fused_computation.80 | loop fusion | bytes 27262976 | tf_op jit(solution)/shard_map/stack | solution.py:82
  126.2 15.2 %fusion.28 = (f32[8,1,64,1024]{3,2,0,1:T(8,128)}, f32[8,1,64,1024]{3,2,0,1:T(8,128)S(1)}, f32[8,1,64,1024]{3,2,0,1:T(8,128)}, f32[8,1,64,1024]{3,2,0,1:T(8,128)}...) fusion(f32[8,64,1024]{2,1,0:T(8,128)S(1)} %bitcast.163), kind=kLoop, calls=%fused_computation.79 | loop fusion | bytes 41943040 | tf_op jit(solution)/shard_map/stack | solution.py:82
  141.4 9.5 %pad_maximum_fusion.7 = (f32[8,4,64,1024]{3,2,0,1:T(8,128)S(1)}, f32[8,4,64,1024]{3,2,0,1:T(8,128)}) fusion(f32[8,1,64,1024]{3,2,0,1:T(8,128)} %get-tuple-element.31, f32[8,1,64,1024]{3,2,0,1:T(8,128)} %get-tuple-element.30, f32[8,1,64,1024]{3,2,0,1:T(8,128)} %get-tuple-element.29, f32[8,1,64,1024]{3,2,0,1:T(8,128)} %get-tuple-element.28, ...), kind=kLoop, calls=%fused_computation.8 | loop fusion | flops 12582912 | bytes 33554432 | tf_op jit(solution)/shard_map/stack | solution.py:82
  152.5 10.8 %pad_maximum_fusion.6 = (f32[8,4,64,1024]{3,2,0,1:T(8,128)}, f32[8,4,64,1024]{3,2,0,1:T(8,128)}) fusion(f32[8,1,64,1024]{3,2,0,1:T(8,128)} %get-tuple-element.26, f32[8,1,64,1024]{3,2,0,1:T(8,128)} %get-tuple-element.25, f32[8,1,64,1024]{3,2,0,1:T(8,128)} %get-tuple-element.24, f32[8,1,64,1024]{3,2,0,1:T(8,128)} %get-tuple-element.23, ...), kind=kLoop, calls=%fused_computation.7 | loop fusion | flops 12582912 | bytes 33554432 | tf_op jit(solution)/shard_map/stack | solution.py:82
  163.3 4.2 %copy.69 = f32[8,4,64,1024]{3,2,1,0:T(8,128)S(1)} copy(f32[8,4,64,1024]{3,2,0,1:T(8,128)} %get-tuple-element.64) | data formatting | bytes 16777216 | tf_op jit(solution)/shard_map/stack | solution.py:82
  167.5 10.8 %pad_maximum_fusion.4 = (f32[8,4,64,1024]{3,2,0,1:T(8,128)}, f32[8,4,64,1024]{3,2,0,1:T(8,128)}) fusion(f32[8,1,64,1024]{3,2,0,1:T(8,128)} %get-tuple-element.18, f32[8,1,64,1024]{3,2,0,1:T(8,128)} %get-tuple-element.17, f32[8,1,64,1024]{3,2,0,1:T(8,128)} %get-tuple-element.16, f32[8,1,64,1024]{3,2,0,1:T(8,128)} %get-tuple-element.15, ...), kind=kLoop, calls=%fused_computation.5 | loop fusion | flops 12582912 | bytes 33554432 | tf_op jit(solution)/shard_map/stack | solution.py:82
  178.3 8.2 %copy.67 = f32[8,4,64,1024]{3,2,1,0:T(8,128)} copy(f32[8,4,64,1024]{3,2,0,1:T(8,128)} %get-tuple-element.62) | data formatting | bytes 16777216 | tf_op jit(solution)/shard_map/stack | solution.py:82
  186.6 10.1 %pad_maximum_fusion.2 = (f32[8,4,64,1024]{3,2,0,1:T(8,128)}, f32[8,4,64,1024]{3,2,0,1:T(8,128)}) fusion(f32[8,1,64,1024]{3,2,0,1:T(8,128)} %get-tuple-element.10, f32[8,1,64,1024]{3,2,0,1:T(8,128)S(1)} %get-tuple-element.9, f32[8,1,64,1024]{3,2,0,1:T(8,128)} %get-tuple-element.38, f32[8,1,64,1024]{3,2,0,1:T(8,128)S(1)} %bitcast.164, ...), kind=kLoop, calls=%fused_computation.3 | loop fusion | flops 12582912 | bytes 33554432 | tf_op jit(solution)/shard_map/stack | solution.py:82
  196.7 8.2 %copy.65 = f32[8,4,64,1024]{3,2,1,0:T(8,128)} copy(f32[8,4,64,1024]{3,2,0,1:T(8,128)} %get-tuple-element.60) | data formatting | bytes 16777216 | tf_op jit(solution)/shard_map/stack | solution.py:82
  205.0 8.3 %copy.66 = f32[8,4,64,1024]{3,2,1,0:T(8,128)} copy(f32[8,4,64,1024]{3,2,0,1:T(8,128)} %get-tuple-element.61) | data formatting | bytes 16777216 | tf_op jit(solution)/shard_map/stack | solution.py:82
  213.2 8.3 %copy.68 = f32[8,4,64,1024]{3,2,1,0:T(8,128)} copy(f32[8,4,64,1024]{3,2,0,1:T(8,128)} %get-tuple-element.63) | data formatting | bytes 16777216 | tf_op jit(solution)/shard_map/stack | solution.py:82
  221.5 8.3 %copy.71 = f32[8,4,64,1024]{3,2,1,0:T(8,128)} copy(f32[8,4,64,1024]{3,2,0,1:T(8,128)} %get-tuple-element.67) | data formatting | bytes 16777216 | tf_op jit(solution)/shard_map/stack | solution.py:82
  229.8 8.3 %copy.72 = f32[8,4,64,1024]{3,2,1,0:T(8,128)} copy(f32[8,4,64,1024]{3,2,0,1:T(8,128)} %get-tuple-element.65) | data formatting | bytes 16777216 | tf_op jit(solution)/shard_map/stack | solution.py:82
  238.0 6.6 %fusion.48 = f32[8,32,1024]{2,1,0:T(8,128)S(1)} fusion(pred[8,32,256]{2,1,0:T(32,128)(4,1)S(1)} %reshape.273, f32[8,256,1024]{2,1,0:T(8,128)} %bitcast.160), kind=kOutput, calls=%fused_computation.127 | convolution fusion | flops 805306368 | bytes 9502720 | tf_op jit(solution)/shard_map/gjx,gxs->gjs/dot_general | solution.py:93
  244.6 6.7 %convolution_add_fusion.6 = f32[8,32,1024]{2,1,0:T(8,128)S(1)} fusion(f32[8,32,1024]{2,1,0:T(8,128)S(1)} %fusion.48, pred[8,32,256]{2,1,0:T(32,128)(4,1)S(1)} %reshape.281, f32[8,256,1024]{2,1,0:T(8,128)} %bitcast.151), kind=kOutput, calls=%fused_computation.104 | convolution fusion | flops 805568512 | bytes 10551296 | tf_op jit(solution)/shard_map/gjx,gxs->gjs/dot_general | solution.py:93
  251.3 3.4 %convolution_add_fusion.5 = f32[8,32,1024]{2,1,0:T(8,128)S(1)} fusion(f32[8,32,1024]{2,1,0:T(8,128)S(1)} %convolution_add_fusion.6, pred[8,32,256]{2,1,0:T(32,128)(4,1)S(1)} %reshape.283, f32[8,256,1024]{2,1,0:T(8,128)S(1)} %bitcast.146), kind=kOutput, calls=%fused_computation.103 | convolution fusion | flops 805568512 | bytes 10551296 | tf_op jit(solution)/shard_map/gjx,gxs->gjs/dot_general | solution.py:93
  254.7 6.5 %convolution_add_fusion.4 = f32[8,32,1024]{2,1,0:T(8,128)S(1)} fusion(f32[8,32,1024]{2,1,0:T(8,128)S(1)} %convolution_add_fusion.5, pred[8,32,256]{2,1,0:T(32,128)(4,1)S(1)} %reshape.285, f32[8,256,1024]{2,1,0:T(8,128)} %bitcast.150), kind=kOutput, calls=%fused_computation.102 | convolution fusion | flops 805568512 | bytes 10551296 | tf_op jit(solution)/shard_map/gjx,gxs->gjs/dot_general | solution.py:93
  261.2 3.2 convolution_add_fusion.3
  267.7 3.4 %convolution_add_fusion.1 = f32[8,32,1024]{2,1,0:T(8,128)S(1)} fusion(f32[8,32,1024]{2,1,0:T(8,128)S(1)} %convolution_add_fusion.2, pred[8,32,256]{2,1,0:T(32,128)(4,1)S(1)} %reshape.291, f32[8,256,1024]{2,1,0:T(8,128)S(1)} %bitcast.149), kind=kOutput, calls=%fused_computation.99 | convolution fusion | flops 805568512 | bytes 10551296 | tf_op jit(solution)/shard_map/gjx,gxs->gjs/dot_general | solution.py:93
  271.1 3.2 fusion.46
  277.1 15.2 %psum.15 = f32[]{:T(128)} all-reduce(f32[]{:T(128)} %multiply_reduce_fusion.2), channel_id=1, replica_groups=mesh['segment'=4,'lane'=8] {'lane'}, use_global_device_ids=true, to_apply=%region_8.9 | all-reduce | flops 1 | bytes 8 | tf_op jit(solution)/shard_map/psum | solution.py:122
  293.0 31.4 %gather_fusion = f32[8192,256]{1,0:T(8,128)} fusion(f32[256,1025]{0,1:T(8,128)S(1)} %concatenate.3, s32[8192]{0:T(1024)S(1)} %bitcast_clamp_fusion), kind=kCustom, calls=%fused_computation | custom fusion | bytes 16809984 | tf_op jit(solution)/shard_map/gather | solution.py:38
  324.4 5.0 %fusion = f32[256,8]{0,1:T(8,128)} fusion(f32[8]{0:T(128)S(1)} %sqrt_multiply_fusion, f32[256,1024]{0,1:T(8,128)S(1)} %pad_slice_fusion.38, f32[8192,256]{1,0:T(8,128)} %gather_fusion), kind=kLoop, calls=%fused_computation.12 | loop fusion | flops 6289408 | bytes 9445408 | tf_op jit(solution)/shard_map/reduce_max | solution.py:41
  (81 shorter events, 31.1 us)
Async XLA Ops:
  40.5 4.1 %copy-start.1 = (s32[64,512]{1,0:T(8,128)S(1)}, s32[64,512]{1,0:T(8,128)}, u32[]{:S(2)}) copy-start(s32[64,512]{1,0:T(8,128)} %param.7) | copy-start | bytes 393220
  46.4 2.2 copy-start
  46.5 8.8 %slice-start.6 = ((s8[8388608]{0:T(1024)(128)(4,1)}), s8[4194304]{0:T(1024)(128)(4,1)S(1)}, s32[]{:S(2)}) async-start(s8[8388608]{0:T(1024)(128)(4,1)} %bitcast.157), calls=%async_computation.7 | async-start | bytes 8388608
  48.7 6.6 %slice-start.7 = ((s8[8388608]{0:T(1024)(128)(4,1)}), s8[4194304]{0:T(1024)(128)(4,1)S(1)}, s32[]{:S(2)}) async-start(s8[8388608]{0:T(1024)(128)(4,1)} %bitcast.157), calls=%async_computation.8 | async-start | bytes 8388608
  61.2 4.2 %copy-start.2 = (s32[256,64]{0,1:T(8,128)S(1)}, s32[256,64]{0,1:T(8,128)}, u32[]{:S(2)}) copy-start(s32[256,64]{0,1:T(8,128)} %param.8) | copy-start | bytes 196612
  61.2 53.1 %all-to-all-start = ((f32[64,8,1024]{2,1,0:T(8,128)}), f32[64,8,1024]{2,1,0:T(8,128)S(1)}, u32[]{:S(2)}, u32[]{:S(2)}) async-start(f32[64,8,1024]{2,1,0:T(8,128)} %copy.62), calls=%async_computation | async-start | bytes 4194304 | tf_op jit(solution)/shard_map/all_to_all | solution.py:119
  66.1 3.0 copy-start.3
  238.0 13.3 %slice-start = ((s8[8388608]{0:T(1024)(128)(4,1)}), s8[4194304]{0:T(1024)(128)(4,1)S(1)}, s32[]{:S(2)}) async-start(s8[8388608]{0:T(1024)(128)(4,1)} %bitcast.144), calls=%async_computation.1 | async-start | bytes 8388608
  244.6 6.7 %slice-start.1 = ((s8[8388608]{0:T(1024)(128)(4,1)}), s8[4194304]{0:T(1024)(128)(4,1)S(1)}, s32[]{:S(2)}) async-start(s8[8388608]{0:T(1024)(128)(4,1)} %bitcast.144), calls=%async_computation.2 | async-start | bytes 8388608
  261.2 6.4 %slice-start.2 = ((s8[8388608]{0:T(1024)(128)(4,1)}), s8[4194304]{0:T(1024)(128)(4,1)S(1)}, s32[]{:S(2)}) async-start(s8[8388608]{0:T(1024)(128)(4,1)} %bitcast.147), calls=%async_computation.3 | async-start | bytes 8388608
  264.4 3.2 slice-start.3
  264.4 6.7 %slice-start.4 = ((s8[8388608]{0:T(1024)(128)(4,1)}), s8[4194304]{0:T(1024)(128)(4,1)S(1)}, s32[]{:S(2)}) async-start(s8[8388608]{0:T(1024)(128)(4,1)} %bitcast.154), calls=%async_computation.5 | async-start | bytes 8388608
  267.6 3.5 %slice-start.5 = ((s8[8388608]{0:T(1024)(128)(4,1)}), s8[4194304]{0:T(1024)(128)(4,1)S(1)}, s32[]{:S(2)}) async-start(s8[8388608]{0:T(1024)(128)(4,1)} %bitcast.154), calls=%async_computation.6 | async-start | bytes 8388608
where the time goes:
time: 336 us; the launch traced here: 330 us
  local copies, waits for them, and re-layouts  137 us (41%)
  other arithmetic  65.5 us (19%)
  waiting for transfers between devices  45.1 us (13%)
  matrix products  42.9 us (13%)
  blocking collectives  33.3 us (10%)
  starting transfers between devices  4.14 us (1%)
    another operation x10, local copies, waits for them, and re-layouts, fine_sums(): jnp.stack([padded[:, :, first_lag + offset:first_lag + offset + samples]...  82.2 us
    all_to_all x1, waiting for transfers between devices, body(): lax.all_to_all(totals, 'lane', split_axis=0, concat_axis=1, tiled=True)  45.1 us
    another operation x4, other arithmetic, fine_sums(): jnp.stack([padded[:, :, first_lag + offset:first_lag + offset + samples]...  41.2 us
    dot_general x8, matrix products, fine_sums(): jnp.einsum('gjx,gxs->gjs', weights, stacked, precision=lax.Precision.HIGH...  36.1 us
    gather x1, local copies, waits for them, and re-layouts, detect(): upper = prefix[:, ends]  31.4 us
    psum x1, blocking collectives, body(): channel_sum = lax.psum(jnp.sum(normed, axis=0), 'lane')  18.1 us
    psum x1, blocking collectives, body(): total_sq = lax.psum(jnp.sum(centered * centered), 'lane')  15.2 us
    another operation x2, local copies, waits for them, and re-layouts, subband_sums(): jnp.stack([padded[:, :, first_lag + offset:first_lag + offset + samples]...  9.6 us
  transfers between devices with their start and end apart: 1, of which 1 were waited for; matrix products, arithmetic and copies ran while one was open for 1% of the time, Pallas kernels for 0%

commit v1 on v0

v1 whole, which is shorter than its diff:
```python
import functools

import jax
import jax.numpy as jnp
from jax import lax
from jax.experimental import pallas as pl
from jax.experimental.pallas import tpu as pltpu
from jax.sharding import PartitionSpec as P

D1 = 8
D2 = 32
LANES = 128

F32 = jnp.float32
BF16 = jnp.bfloat16


def iota(shape, axis):
    return lax.broadcasted_iota(jnp.int32, shape, axis)


def split(x):
    hi = x.astype(BF16)
    lo = (x - hi.astype(F32)).astype(BF16)
    return hi, lo


def dot(a, b):
    return lax.dot_general(a, b, (((1,), (0,)), ((), ())), preferred_element_type=F32)


def hot(mask):
    return jnp.where(mask, 1.0, 0.0).astype(BF16)


def shift_lanes(x, by):
    if by == 0:
        return x
    rolled = pltpu.roll(x, LANES - by, 1)
    return jnp.where(iota(x.shape, 1) < LANES - by, rolled, 0.0)


def search_kernel(
    cfg,
    spectra,
    flags,
    sub_delay,
    fine_delay,
    centered_ref,
    total_ref,
    power,
    flag_rows,
    normed,
    perm,
    delays2,
    wc,
    xs,
    out_blocks,
    incoming,
    fine_rep,
    wf,
    zmine,
    zall,
    smine,
    sall,
    in_sems,
    own_sems,
    send_sems,
    recv_sems,
    zsend,
    zrecv,
    ssend,
    srecv,
):
    lanes, R, NB, SUB, CD, NH, QC, QF, NSUB, PER = cfg
    KC = CD // NH
    samples = R * LANES
    rows = NB * SUB
    me = lax.axis_index("lane")
    batch = lax.axis_index("segment")

    load_power = pltpu.make_async_copy(spectra.at[batch], power, in_sems.at[0])
    load_flags = pltpu.make_async_copy(flags.at[batch], flag_rows, in_sems.at[1])
    load_power.start()
    load_flags.start()

    def peer(step):
        return lax.rem(me + step, lanes)

    barrier = pltpu.get_barrier_semaphore()
    for step in range(1, lanes):
        pl.semaphore_signal(barrier, inc=1, device_id={"lane": peer(step)}, device_id_type=pl.DeviceIdType.MESH)

    for r in range(R):
        src = R * iota((samples, LANES), 1) + r
        perm[:, r * LANES : (r + 1) * LANES] = hot(iota((samples, LANES), 0) == src)

    load_power.wait()
    load_flags.wait()

    blocks = flag_rows.shape[1]
    width = samples // blocks
    row_step = min(64, rows)

    def clean(g, _):
        sl = pl.ds(pl.multiple_of(g * row_step, row_step), row_step)
        kept = 1.0 - flag_rows[sl, :].astype(F32)
        mask = jnp.concatenate(
            [jnp.broadcast_to(kept[:, n : n + 1], (row_step, width)) for n in range(blocks)], axis=1
        )
        x = power[sl, :]
        masked = mask * x
        centre = jnp.sum(masked, axis=1, keepdims=True) * (1.0 / samples)
        off = masked - centre
        spread = jnp.sum(off * off, axis=1, keepdims=True) * (1.0 / samples)
        out = mask * (x - centre) * lax.rsqrt(spread + 1e-05)
        hi, lo = split(out)
        both = dot(jnp.concatenate([hi, lo], axis=0), perm[...])
        normed[sl, :] = both[:row_step] + both[row_step:]
        return _

    lax.fori_loop(0, rows // row_step, clean, 0)

    for r in range(R):
        zmine[r : r + 1, :] = jnp.sum(normed[:, r * LANES : (r + 1) * LANES], axis=0, keepdims=True)
    zall[me] = zmine[...]
    pl.semaphore_wait(barrier, lanes - 1)

    def z_copy(step):
        return pltpu.make_async_remote_copy(
            zmine, zall.at[me], zsend.at[step], zrecv.at[step],
            device_id={"lane": peer(step)}, device_id_type=pl.DeviceIdType.MESH,
        )

    for step in range(1, lanes):
        z_copy(step).start()

    per_tile = LANES // SUB
    for b in range(NB):
        block = sub_delay[:, b * SUB : (b + 1) * SUB]
        delays2[b] = jnp.concatenate([block] * per_tile, axis=1)

    def coarse_weights(b, _):
        d = delays2[b]
        d = jnp.broadcast_to(d[:, None, :], (lanes * CD, R, LANES)).reshape(lanes, NH, KC, R, LANES)
        for h in range(NH):
            part = d[:, h].reshape(lanes * KC, R, LANES)
            for q in range(QC):
                for lt in range(R * SUB // LANES):
                    lag = R * q + lt * per_tile + iota((R, LANES), 1) // SUB - iota((R, LANES), 0)
                    n = lanes * KC * R
                    wc[b, h, q * n : (q + 1) * n, lt * LANES : (lt + 1) * LANES] = hot(part == lag[None]).reshape(n, LANES)
        return _

    lax.fori_loop(0, NB, coarse_weights, 0)

    for step in range(1, lanes):
        z_copy(step).wait()
    zero = zall[0]
    for e in range(1, lanes):
        zero = zero + zall[e]
    zmean = zero * (1.0 / (lanes * rows))

    def prepare(b, _):
        sl = pl.ds(pl.multiple_of(b * SUB, SUB), SUB)
        for r in range(R):
            part = normed[sl, r * LANES : (r + 1) * LANES] - zmean[r : r + 1, :]
            hi, lo = split(part)
            xs[b, r * SUB : (r + 1) * SUB, :LANES] = hi
            xs[b, r * SUB : (r + 1) * SUB, LANES:] = lo
        return _

    lax.fori_loop(0, NB, prepare, 0)

    def block_copy(step, h):
        e = peer(step)
        return pltpu.make_async_remote_copy(
            out_blocks.at[h, e],
            incoming.at[h, :, pl.ds(me * NB, NB)],
            send_sems.at[step, h],
            recv_sems.at[step, h],
            device_id={"lane": e},
            device_id_type=pl.DeviceIdType.MESH,
        )

    def own_copy(h):
        return pltpu.make_async_copy(
            out_blocks.at[h, me], incoming.at[h, :, pl.ds(me * NB, NB)], own_sems.at[h]
        )

    for h in range(NH):

        def coarse(b, _):
            n = lanes * KC * R
            o = dot(wc[b, h], xs[b])
            o = o[:, :LANES] + o[:, LANES:]
            total = o[:n]
            for q in range(1, QC):
                total = total + shift_lanes(o[q * n : (q + 1) * n], q)
            out_blocks[h, :, :, b] = total.reshape(lanes, KC, R, LANES)
            return _

        lax.fori_loop(0, NB, coarse, 0)
        for step in range(1, lanes):
            block_copy(step, h).start()
        own_copy(h).start()

    cols = NSUB * R
    rep = hot(iota((NSUB, cols), 1) // R == iota((NSUB, cols), 0))
    fine_rep[...] = dot(fine_delay[...].astype(F32).astype(BF16), rep).astype(jnp.int32)

    def fine_weights(k, _):
        sl = pl.ds(pl.multiple_of(k * PER, PER), PER)
        for lt in range(cols // LANES):
            d = fine_rep[sl, lt * LANES : (lt + 1) * LANES]
            d = jnp.broadcast_to(d[:, None, :], (PER, R, LANES))
            for q in range(QF):
                lag = R * q + iota((R, LANES), 1) % R - iota((R, LANES), 0)
                n = PER * R
                wf[k, q * n : (q + 1) * n, lt * LANES : (lt + 1) * LANES] = hot(d == lag[None]).reshape(n, LANES)
        return _

    lax.fori_loop(0, CD, fine_weights, 0)

    smine[...] = jnp.zeros_like(smine)
    for h in range(NH):
        own_copy(h).wait()
        for step in range(1, lanes):
            block_copy(step, h).wait_recv()

        def fine(kl, _):
            k = h * KC + kl
            n = PER * R
            hi, lo = split(incoming[h, kl].reshape(NSUB * R, LANES))
            o = dot(wf[k], jnp.concatenate([hi, lo], axis=1))
            o = o[:, :LANES] + o[:, LANES:]
            total = o[:n]
            for q in range(1, QF):
                total = total + shift_lanes(o[q * n : (q + 1) * n], q)
            series = total.reshape(PER, R, LANES)
            mean = jnp.sum(jnp.sum(series, axis=1, keepdims=True), axis=2, keepdims=True) * (1.0 / samples)
            series = series - mean
            centered_ref[pl.ds(k * PER, PER)] = series
            smine[...] += jnp.sum(series * series, axis=0)
            return _

        lax.fori_loop(0, KC, fine, 0)

    sall[me] = smine[...]

    def s_copy(step):
        return pltpu.make_async_remote_copy(
            smine, sall.at[me], ssend.at[step], srecv.at[step],
            device_id={"lane": peer(step)}, device_id_type=pl.DeviceIdType.MESH,
        )

    for step in range(1, lanes):
        s_copy(step).start()
    for h in range(NH):
        for step in range(1, lanes):
            block_copy(step, h).wait_send()
    for step in range(1, lanes):
        s_copy(step).wait()
    total = sall[0]
    for e in range(1, lanes):
        total = total + sall[e]
    total_ref[...] = total


def detect_kernel(count, x_ref, total_ref, widths_ref, wrow_ref, out_ref, best):
    trials, R, L = x_ref.shape
    samples = R * L
    nw = widths_ref.shape[0]
    step = min(32, trials)
    upper_tri = hot(iota((L, L), 0) < iota((L, L), 1))

    def body(g, _):
        sl = pl.ds(pl.multiple_of(g * step, step), step)
        x = x_ref[sl]
        flat = x.reshape(step * R, L)
        hi = flat.astype(BF16)
        rest = flat - hi.astype(F32)
        mid = rest.astype(BF16)
        lo = (rest - mid.astype(F32)).astype(BF16)
        before = dot(hi, upper_tri) + dot(mid, upper_tri) + dot(lo, upper_tri)
        before = jnp.sum(before.reshape(step, R, L), axis=1, keepdims=True)
        sub = iota((step, R, L), 1)
        lane = iota((step, R, L), 2)
        run = x
        hop = 1
        while hop < R:
            run = run + jnp.where(sub >= hop, pltpu.roll(run, hop, 1), 0.0)
            hop *= 2
        prefix = before + run - x
        whole = jnp.sum(jnp.sum(x, axis=1, keepdims=True), axis=2, keepdims=True)
        pos = R * lane + sub
        for wi in range(nw):
            w = widths_ref[wi]
            a = w // R
            b = w - a * R
            y = pltpu.roll(prefix, lax.rem(R - b, R), 1)
            y = pltpu.roll(y.reshape(step * R, L), lax.rem(L - a, L), 1)
            y1 = pltpu.roll(y, L - 1, 1).reshape(step, R, L)
            y = jnp.where(sub + b >= R, y1, y.reshape(step, R, L))
            y = jnp.where(pos + w >= samples, whole, y)
            best[wi, sl, :] = jnp.max(y - prefix, axis=1)
        return _

    lax.fori_loop(0, trials // step, body, 0)
    sigma = jnp.sqrt(jnp.sum(total_ref[...], axis=(0, 1), keepdims=True) * (1.0 / count) + 1e-06)
    out = jnp.zeros((trials, LANES), F32)
    for wi in range(nw):
        top = jnp.max(best[wi], axis=1, keepdims=True)
        out = jnp.where(iota((trials, LANES), 1) == wi, top, out)
    scale = sigma * jnp.sqrt(wrow_ref[...].astype(F32))
    out_ref[0] = out[:, :nw] / scale


def body(lanes, spectra, rfi_flags, sub_delay, fine_delay, widths):
    batches, rows, samples = spectra.shape
    R = samples // LANES
    coarse = sub_delay.shape[0]
    trials, NSUB = fine_delay.shape
    SUB = rows * lanes // NSUB
    NB = rows // SUB
    CD = coarse // lanes
    PER = trials // CD
    NH = min(4, CD)
    KC = CD // NH
    QC = (R - 1 + D1 - 1) // R + 1
    QF = (R - 1 + D2 - 1) // R + 1
    cfg = (lanes, R, NB, SUB, CD, NH, QC, QF, NSUB, PER)
    any_spec = pl.BlockSpec(memory_space=pl.ANY)
    vmem = pl.BlockSpec(memory_space=pltpu.VMEM)
    dma = pltpu.SemaphoreType.DMA
    centered, total = pl.pallas_call(
        functools.partial(search_kernel, cfg),
        out_shape=(
            jax.ShapeDtypeStruct((trials, R, LANES), F32),
            jax.ShapeDtypeStruct((R, LANES), F32),
        ),
        in_specs=[any_spec, any_spec, vmem, vmem],
        out_specs=(vmem, vmem),
        scratch_shapes=[
            pltpu.VMEM((rows, samples), F32),
            pltpu.VMEM((rows, rfi_flags.shape[2]), jnp.int32),
            pltpu.VMEM((rows, samples), F32),
            pltpu.VMEM((samples, samples), BF16),
            pltpu.VMEM((NB, coarse, LANES), jnp.int32),
            pltpu.VMEM((NB, NH, QC * lanes * KC * R, R * SUB), BF16),
            pltpu.VMEM((NB, R * SUB, 2 * LANES), BF16),
            pltpu.VMEM((NH, lanes, KC, NB, R, LANES), F32),
            pltpu.VMEM((NH, KC, NSUB, R, LANES), F32),
            pltpu.VMEM((trials, NSUB * R), jnp.int32),
            pltpu.VMEM((CD, QF * PER * R, NSUB * R), BF16),
            pltpu.VMEM((R, LANES), F32),
            pltpu.VMEM((lanes, R, LANES), F32),
            pltpu.VMEM((R, LANES), F32),
            pltpu.VMEM((lanes, R, LANES), F32),
            dma((2,)),
            dma((NH,)),
            dma((lanes, NH)),
            dma((lanes, NH)),
            dma((lanes,)),
            dma((lanes,)),
            dma((lanes,)),
            dma((lanes,)),
        ],
        compiler_params=pltpu.CompilerParams(
            collective_id=0, has_side_effects=True, vmem_limit_bytes=60 * 1024 * 1024
        ),
    )(spectra, rfi_flags, sub_delay, fine_delay)
    nw = widths.shape[0]
    return pl.pallas_call(
        functools.partial(detect_kernel, trials * lanes * samples),
        out_shape=jax.ShapeDtypeStruct((1, trials, nw), F32),
        in_specs=[vmem, vmem, pl.BlockSpec(memory_space=pltpu.SMEM), vmem],
        out_specs=vmem,
        scratch_shapes=[pltpu.VMEM((nw, trials, LANES), F32)],
    )(centered, total, widths, widths.reshape(1, nw))


def solution(mesh):
    in_specs = (P(None, "lane", None), P(None, "lane", None), P(None, "lane"), P("lane", None), P())
    out_specs = P("segment", "lane", None)
    return jax.shard_map(
        functools.partial(body, mesh.shape["lane"]),
        mesh=mesh, in_specs=in_specs, out_specs=out_specs, check_vma=False,
    )
```

time: 336 us -> 87.2 us (0.26); the launches traced: 330 us -> 86.9 us
  local copies, waits for them, and re-layouts: 137 us -> 5.38 us
  Pallas kernels: 0 us -> 81.5 us
  other arithmetic: 65.5 us -> 0 us
  waiting for transfers between devices: 45.1 us -> 0 us
  matrix products: 42.9 us -> 0 us
  blocking collectives: 33.3 us -> 0 us
  starting transfers between devices: 4.14 us -> 0 us
    another operation x15 -> x0, local copies, waits for them, and re-layouts: 92.1 us -> none  [the longest x10 82.2 us: fine_sums(): jnp.stack([padded[:, :, first_lag + offset:first_lag + offset + samples]...]
    pallas_call x0 -> x2, Pallas kernels: none -> 81.5 us  [the longest x1 71.4 us: body(): pl.pallas_call(functools.partial(search_kernel, cfg), out_shape=(jax.Shap...]
    another operation x9 -> x0, other arithmetic: 45.9 us -> none  [the longest x4 41.2 us: fine_sums(): jnp.stack([padded[:, :, first_lag + offset:first_lag + offset + samples]...]
    all_to_all x1 -> x0, waiting for transfers between devices: 45.1 us -> none  [body(): lax.all_to_all(totals, 'lane', split_axis=0, concat_axis=1, tiled=True)]
    dot_general x10 -> x0, matrix products: 42.9 us -> none  [the longest x8 36.1 us: fine_sums(): jnp.einsum('gjx,gxs->gjs', weights, stacked, precision=lax.Precision.HIGH...]
    psum x2 -> x0, blocking collectives: 33.3 us -> none  [the longest x1 18.1 us: body(): channel_sum = lax.psum(jnp.sum(normed, axis=0), 'lane')]
    gather x1 -> x0, local copies, waits for them, and re-layouts: 31.4 us -> none  [detect(): upper = prefix[:, ends]]
    reduce_sum x4 -> x0, other arithmetic: 8.65 us -> none  [the longest x1 3.8 us: clean_block(): centre = jnp.mean(masked, axis=1, keepdims=True)]
  transfers between devices with their start and end apart: 1 -> 0, of which waited for: 1 -> 0; matrix products, arithmetic and copies ran while one was open for 1% -> 0% of each run, Pallas kernels for 0% -> 0%
where the time goes in v1:
time: 87.2 us; the launch traced here: 86.9 us
  Pallas kernels  81.5 us (93%)
  local copies, waits for them, and re-layouts  5.38 us (6%)
    pallas_call x1, Pallas kernels, body(): pl.pallas_call(functools.partial(search_kernel, cfg), out_shape=(jax.Shap...  71.4 us
    pallas_call x1, Pallas kernels, body(): pl.pallas_call(functools.partial(detect_kernel, trials * lanes * samples)...  10.1 us
    unnamed x2, local copies, waits for them, and re-layouts  3.81 us

profile of v1, /device:TPU:0, one launch (start us, length us, event | category | flops | bytes accessed | tf_op | source)
XLA Modules:
  0.0 86.9 jit_solution(3374786196667943317)
XLA Ops:
  0.0 1.6 %copy.7.fine_delay = s32[256,64]{1,0:T(8,128)} copy(s32[256,64]{0,1:T(8,128)} %param.8) | data formatting | bytes 131072 | tf_op args[3]
  1.6 2.2 %copy.6.flags = s32[4,512,8]{2,1,0:T(8,128)} copy(s32[4,512,8]{1,2,0:T(8,128)} %param.6) | data formatting | bytes 131072 | tf_op args[1]
  3.8 71.4 %shard_map.55 = (f32[256,8,128]{2,1,0:T(8,128)}, f32[8,128]{1,0:T(8,128)}) custom-call(f32[4,512,1024]{2,1,0:T(8,128)} %spectra.1, s32[4,512,8]{2,1,0:T(8,128)} %copy.6.flags, s32[64,512]{1,0:T(8,128)} %sub_delay.1, s32[256,64]{1,0:T(8,128)} %copy.7.fine_delay), custom_call_target="tpu_custom_call" | custom-call | tf_op jit(solution)/shard_map/pallas_call | solution.py:336
  75.2 10.1 %shard_map.56 = f32[1,256,8]{2,1,0:T(8,128)} custom-call(f32[256,8,128]{2,1,0:T(8,128)} %get-tuple-element.7.x_ref, f32[8,128]{1,0:T(8,128)} %get-tuple-element.8.total_ref, s32[8]{0:T(128)} %widths_ref.1, s32[1,8]{1,0:T(1,128)} %bitcast.1), custom_call_target="tpu_custom_call" | custom-call | tf_op jit(solution)/shard_map/pallas_call | solution.py:374
  85.3 1.6 %copy.8 = f32[1,256,8]{1,2,0:T(8,128)} copy(f32[1,256,8]{2,1,0:T(8,128)} %shard_map.56) | data formatting | bytes 16384 | tf_op jit(solution)/shard_map/pallas_call | solution.py:374

commit v2 on v1

--- a/solution.py
+++ b/solution.py
@@ -9,6 +9,7 @@
 
 D1 = 8
 D2 = 32
+WMAX = 64
 LANES = 128
 
 F32 = jnp.float32
@@ -38,6 +39,48 @@
         return x
     rolled = pltpu.roll(x, LANES - by, 1)
     return jnp.where(iota(x.shape, 1) < LANES - by, rolled, 0.0)
+
+
+def shift_samples(x, by):
+    n, R, L = x.shape
+    if by % R == 0:
+        return pltpu.roll(x.reshape(n * R, L), L - by // R, 1).reshape(n, R, L)
+    y = pltpu.roll(x, R - by, 1)
+    y1 = pltpu.roll(y.reshape(n * R, L), L - 1, 1).reshape(n, R, L)
+    return jnp.where(iota((1, R, L), 1) >= R - by, y1, y)
+
+
+def boxcars(x, widths_ref):
+    n, R, L = x.shape
+    upper_tri = hot(iota((L, L), 0) < iota((L, L), 1))
+    flat = x.reshape(n * R, L)
+    hi = flat.astype(BF16)
+    rest = flat - hi.astype(F32)
+    mid = rest.astype(BF16)
+    lo = (rest - mid.astype(F32)).astype(BF16)
+    before = dot(hi, upper_tri) + dot(mid, upper_tri) + dot(lo, upper_tri)
+    before = jnp.sum(before.reshape(n, R, L), axis=1, keepdims=True)
+    sub = iota((1, R, L), 1)
+    pos = R * iota((1, R, L), 2) + sub
+    run = x
+    hop = 1
+    while hop < R:
+        run = run + jnp.where(sub >= hop, pltpu.roll(run, hop, 1), 0.0)
+        hop *= 2
+    prefix = before + run - x
+    whole = jnp.sum(jnp.sum(x, axis=1, keepdims=True), axis=2, keepdims=True)
+    out = jnp.zeros((n, LANES), F32)
+    for wi in range(widths_ref.shape[0]):
+        w = jnp.full((1, R, L), widths_ref[wi], jnp.int32)
+        y = prefix
+        by = 1
+        while by <= WMAX:
+            y = jnp.where((w & by) != 0, shift_samples(y, by), y)
+            by *= 2
+        y = jnp.where(pos + w >= R * L, whole, y)
+        top = jnp.max(jnp.max(y - prefix, axis=1), axis=1, keepdims=True)
+        out = jnp.where(iota((n, LANES), 1) == wi, top, out)
+    return out
 
 
 def search_kernel(
@@ -46,12 +89,15 @@
     flags,
     sub_delay,
     fine_delay,
-    centered_ref,
-    total_ref,
+    widths_ref,
+    tops_ref,
+    sigma_ref,
     power,
     flag_rows,
+    tops,
     normed,
     perm,
+    kept_all,
     delays2,
     wc,
     xs,
@@ -79,10 +125,17 @@
     me = lax.axis_index("lane")
     batch = lax.axis_index("segment")
 
-    load_power = pltpu.make_async_copy(spectra.at[batch], power, in_sems.at[0])
-    load_flags = pltpu.make_async_copy(flags.at[batch], flag_rows, in_sems.at[1])
-    load_power.start()
+    row_step = min(64, rows)
+    steps = rows // row_step
+
+    def load(g):
+        sl = pl.ds(pl.multiple_of(g * row_step, row_step), row_step)
+        return pltpu.make_async_copy(spectra.at[batch, sl], power.at[sl], in_sems.at[g])
+
+    load_flags = pltpu.make_async_copy(flags.at[batch], flag_rows, in_sems.at[steps])
     load_flags.start()
+    for g in range(steps):
+        load(g).start()
 
     def peer(step):
         return lax.rem(me + step, lanes)
@@ -91,20 +144,22 @@
     for step in range(1, lanes):
         pl.semaphore_signal(barrier, inc=1, device_id={"lane": peer(step)}, device_id_type=pl.DeviceIdType.MESH)
 
-    for r in range(R):
-        src = R * iota((samples, LANES), 1) + r
-        perm[:, r * LANES : (r + 1) * LANES] = hot(iota((samples, LANES), 0) == src)
-
-    load_power.wait()
+    pair = 2 * LANES
+    chunk = pair // R
+    per_lane_tile = LANES // chunk
+    col = iota((pair, pair), 1)
+    perm[...] = hot(iota((pair, pair), 0) == R * (col % chunk) + col // chunk)
+    lane_row = iota((1, LANES), 1)
+
     load_flags.wait()
-
-    blocks = flag_rows.shape[1]
+    blocks = flag_rows.shape[0]
     width = samples // blocks
-    row_step = min(64, rows)
+    kept_all[...] = 1.0 - flag_rows[...].astype(F32).T
 
     def clean(g, _):
         sl = pl.ds(pl.multiple_of(g * row_step, row_step), row_step)
-        kept = 1.0 - flag_rows[sl, :].astype(F32)
+        load(g).wait()
+        kept = kept_all[sl, :]
         mask = jnp.concatenate(
             [jnp.broadcast_to(kept[:, n : n + 1], (row_step, width)) for n in range(blocks)], axis=1
         )
@@ -115,11 +170,23 @@
         spread = jnp.sum(off * off, axis=1, keepdims=True) * (1.0 / samples)
         out = mask * (x - centre) * lax.rsqrt(spread + 1e-05)
         hi, lo = split(out)
-        both = dot(jnp.concatenate([hi, lo], axis=0), perm[...])
-        normed[sl, :] = both[:row_step] + both[row_step:]
+        both = jnp.concatenate([hi, lo], axis=0)
+        pieces = []
+        for p in range(samples // pair):
+            o = dot(both[:, p * pair : (p + 1) * pair], perm[...])
+            pieces.append(o[:row_step] + o[row_step:])
+        for r in range(R):
+            tile, at = r // per_lane_tile, r % per_lane_tile * chunk
+            dest = None
+            for p, o in enumerate(pieces):
+                x = o[:, tile * LANES : (tile + 1) * LANES]
+                move = (p * chunk - at) % LANES
+                x = pltpu.roll(x, move, 1) if move else x
+                dest = x if dest is None else jnp.where(lane_row >= p * chunk, x, dest)
+            normed[sl, r * LANES : (r + 1) * LANES] = dest
         return _
 
-    lax.fori_loop(0, rows // row_step, clean, 0)
+    lax.fori_loop(0, steps, clean, 0)
 
     for r in range(R):
         zmine[r : r + 1, :] = jnp.sum(normed[:, r * LANES : (r + 1) * LANES], axis=0, keepdims=True)
@@ -207,7 +274,7 @@
 
     cols = NSUB * R
     rep = hot(iota((NSUB, cols), 1) // R == iota((NSUB, cols), 0))
-    fine_rep[...] = dot(fine_delay[...].astype(F32).astype(BF16), rep).astype(jnp.int32)
+    fine_rep[...] = dot(fine_delay[...].astype(F32).T.astype(BF16), rep).astype(jnp.int32)
 
     def fine_weights(k, _):
         sl = pl.ds(pl.multiple_of(k * PER, PER), PER)
@@ -240,7 +307,7 @@
             series = total.reshape(PER, R, LANES)
             mean = jnp.sum(jnp.sum(series, axis=1, keepdims=True), axis=2, keepdims=True) * (1.0 / samples)
             series = series - mean
-            centered_ref[pl.ds(k * PER, PER)] = series
+            tops[pl.ds(pl.multiple_of(k * PER, PER), PER), :] = boxcars(series, widths_ref)
             smine[...] += jnp.sum(series * series, axis=0)
             return _
 
@@ -264,56 +331,10 @@
     total = sall[0]
     for e in range(1, lanes):
         total = total + sall[e]
-    total_ref[...] = total
-
-
-def detect_kernel(count, x_ref, total_ref, widths_ref, wrow_ref, out_ref, best):
-    trials, R, L = x_ref.shape
-    samples = R * L
-    nw = widths_ref.shape[0]
-    step = min(32, trials)
-    upper_tri = hot(iota((L, L), 0) < iota((L, L), 1))
-
-    def body(g, _):
-        sl = pl.ds(pl.multiple_of(g * step, step), step)
-        x = x_ref[sl]
-        flat = x.reshape(step * R, L)
-        hi = flat.astype(BF16)
-        rest = flat - hi.astype(F32)
-        mid = rest.astype(BF16)
-        lo = (rest - mid.astype(F32)).astype(BF16)
-        before = dot(hi, upper_tri) + dot(mid, upper_tri) + dot(lo, upper_tri)
-        before = jnp.sum(before.reshape(step, R, L), axis=1, keepdims=True)
-        sub = iota((step, R, L), 1)
-        lane = iota((step, R, L), 2)
-        run = x
-        hop = 1
-        while hop < R:
-            run = run + jnp.where(sub >= hop, pltpu.roll(run, hop, 1), 0.0)
-            hop *= 2
-        prefix = before + run - x
-        whole = jnp.sum(jnp.sum(x, axis=1, keepdims=True), axis=2, keepdims=True)
-        pos = R * lane + sub
-        for wi in range(nw):
-            w = widths_ref[wi]
-            a = w // R
-            b = w - a * R
-            y = pltpu.roll(prefix, lax.rem(R - b, R), 1)
-            y = pltpu.roll(y.reshape(step * R, L), lax.rem(L - a, L), 1)
-            y1 = pltpu.roll(y, L - 1, 1).reshape(step, R, L)
-            y = jnp.where(sub + b >= R, y1, y.reshape(step, R, L))
-            y = jnp.where(pos + w >= samples, whole, y)
-            best[wi, sl, :] = jnp.max(y - prefix, axis=1)
-        return _
-
-    lax.fori_loop(0, trials // step, body, 0)
-    sigma = jnp.sqrt(jnp.sum(total_ref[...], axis=(0, 1), keepdims=True) * (1.0 / count) + 1e-06)
-    out = jnp.zeros((trials, LANES), F32)
-    for wi in range(nw):
-        top = jnp.max(best[wi], axis=1, keepdims=True)
-        out = jnp.where(iota((trials, LANES), 1) == wi, top, out)
-    scale = sigma * jnp.sqrt(wrow_ref[...].astype(F32))
-    out_ref[0] = out[:, :nw] / scale
+    total = jnp.sum(jnp.sum(total, axis=0, keepdims=True), axis=1, keepdims=True)
+    sigma = jnp.sqrt(total * (1.0 / (lanes * CD * PER * samples)) + 1e-06)
+    tops_ref[...] = tops[...].T[: tops_ref.shape[0]]
+    sigma_ref[...] = jnp.broadcast_to(sigma, sigma_ref.shape)
 
 
 def body(lanes, spectra, rfi_flags, sub_delay, fine_delay, widths):
@@ -325,7 +346,7 @@
     NB = rows // SUB
     CD = coarse // lanes
     PER = trials // CD
-    NH = min(4, CD)
+    NH = min(8, CD)
     KC = CD // NH
     QC = (R - 1 + D1 - 1) // R + 1
     QF = (R - 1 + D2 - 1) // R + 1
@@ -333,19 +354,22 @@
     any_spec = pl.BlockSpec(memory_space=pl.ANY)
     vmem = pl.BlockSpec(memory_space=pltpu.VMEM)
     dma = pltpu.SemaphoreType.DMA
-    centered, total = pl.pallas_call(
+    nw = widths.shape[0]
+    tops, sigma = pl.pallas_call(
         functools.partial(search_kernel, cfg),
         out_shape=(
-            jax.ShapeDtypeStruct((trials, R, LANES), F32),
-            jax.ShapeDtypeStruct((R, LANES), F32),
+            jax.ShapeDtypeStruct((nw, trials), F32),
+            jax.ShapeDtypeStruct((nw, trials), F32),
         ),
-        in_specs=[any_spec, any_spec, vmem, vmem],
+        in_specs=[any_spec, any_spec, vmem, vmem, pl.BlockSpec(memory_space=pltpu.SMEM)],
         out_specs=(vmem, vmem),
         scratch_shapes=[
             pltpu.VMEM((rows, samples), F32),
-            pltpu.VMEM((rows, rfi_flags.shape[2]), jnp.int32),
+            pltpu.VMEM((rfi_flags.shape[2], rows), jnp.int32),
+            pltpu.VMEM((trials, LANES), F32),
             pltpu.VMEM((rows, samples), F32),
-            pltpu.VMEM((samples, samples), BF16),
+            pltpu.VMEM((2 * LANES, 2 * LANES), BF16),
+            pltpu.VMEM((rows, rfi_flags.shape[2]), F32),
             pltpu.VMEM((NB, coarse, LANES), jnp.int32),
             pltpu.VMEM((NB, NH, QC * lanes * KC * R, R * SUB), BF16),
             pltpu.VMEM((NB, R * SUB, 2 * LANES), BF16),
@@ -357,7 +381,7 @@
             pltpu.VMEM((lanes, R, LANES), F32),
             pltpu.VMEM((R, LANES), F32),
             pltpu.VMEM((lanes, R, LANES), F32),
-            dma((2,)),
+            dma((rows // min(64, rows) + 1,)),
             dma((NH,)),
             dma((lanes, NH)),
             dma((lanes, NH)),
@@ -369,15 +393,9 @@
         compiler_params=pltpu.CompilerParams(
             collective_id=0, has_side_effects=True, vmem_limit_bytes=60 * 1024 * 1024
         ),
-    )(spectra, rfi_flags, sub_delay, fine_delay)
-    nw = widths.shape[0]
-    return pl.pallas_call(
-        functools.partial(detect_kernel, trials * lanes * samples),
-        out_shape=jax.ShapeDtypeStruct((1, trials, nw), F32),
-        in_specs=[vmem, vmem, pl.BlockSpec(memory_space=pltpu.SMEM), vmem],
-        out_specs=vmem,
-        scratch_shapes=[pltpu.VMEM((nw, trials, LANES), F32)],
-    )(centered, total, widths, widths.reshape(1, nw))
+    )(spectra, rfi_flags.transpose(0, 2, 1), sub_delay, fine_delay.T, widths)
+    peaks = tops / (sigma * jnp.sqrt(widths.astype(F32))[:, None])
+    return peaks.T[None]
 
 
 def solution(mesh):

time: 87.2 us -> 77.9 us (0.89)
  Pallas kernels: 81.5 us -> 75.5 us
  local copies, waits for them, and re-layouts: 5.38 us -> 0 us
  other arithmetic: 0 us -> 2.05 us
    pallas_call x1 -> x0, Pallas kernels: 10.1 us -> none  [body(): pl.pallas_call(functools.partial(detect_kernel, trials * lanes * samples)...]
    pallas_call x1, Pallas kernels: 71.4 us -> 75.5 us  [body(): pl.pallas_call(functools.partial(search_kernel, cfg), out_shape=(jax.Shap...]
    unnamed x2 -> x0, local copies, waits for them, and re-layouts: 3.81 us -> none
    pallas_call x1 -> x0, local copies, waits for them, and re-layouts: 1.57 us -> none  [body(): pl.pallas_call(functools.partial(detect_kernel, trials * lanes * samples)...]
    broadcast_in_dim x0 -> x1, other arithmetic: none -> 1.39 us  [body(): return peaks.T[None]]
where the time goes in v2:
time: 77.9 us; the launch traced here: 77.6 us
  Pallas kernels  75.5 us (97%)
  other arithmetic  2.05 us (3%)
    pallas_call x1, Pallas kernels, body(): pl.pallas_call(functools.partial(search_kernel, cfg), out_shape=(jax.Shap...  75.5 us

profile of v2, /device:TPU:0, one launch (start us, length us, event | category | flops | bytes accessed | tf_op | source)
XLA Modules:
  0.0 77.6 jit_solution(6514617976130434388)
XLA Ops:
  0.0 0.7 convert_sqrt_fusion
  0.7 75.5 %shard_map.55 = (f32[8,256]{1,0:T(8,128)}, f32[8,256]{1,0:T(8,128)}) custom-call(f32[4,512,1024]{2,1,0:T(8,128)} %spectra.1, s32[4,8,512]{2,1,0:T(8,128)} %bitcast.6, s32[64,512]{1,0:T(8,128)} %sub_delay.1, s32[64,256]{1,0:T(8,128)} %bitcast.7, s32[8]{0:T(128)} %widths_ref.1), custom_call_target="tpu_custom_call" | custom-call | tf_op jit(solution)/shard_map/pallas_call | solution.py:358
  76.2 1.4 %divide_bitcast_fusion = f32[1,256,8]{1,2,0:T(8,128)} fusion(f32[8,256]{1,0:T(8,128)} %get-tuple-element.7, f32[8,256]{1,0:T(8,128)} %get-tuple-element.8, f32[8]{0:T(128)S(1)} %convert_sqrt_fusion), kind=kLoop, calls=%fused_computation | loop fusion | flops 4096 | bytes 24608 | tf_op jit(solution)/shard_map/broadcast_in_dim | solution.py:398

commit v3 on v2

--- a/solution.py
+++ b/solution.py
@@ -41,16 +41,7 @@
     return jnp.where(iota(x.shape, 1) < LANES - by, rolled, 0.0)
 
 
-def shift_samples(x, by):
-    n, R, L = x.shape
-    if by % R == 0:
-        return pltpu.roll(x.reshape(n * R, L), L - by // R, 1).reshape(n, R, L)
-    y = pltpu.roll(x, R - by, 1)
-    y1 = pltpu.roll(y.reshape(n * R, L), L - 1, 1).reshape(n, R, L)
-    return jnp.where(iota((1, R, L), 1) >= R - by, y1, y)
-
-
-def boxcars(x, widths_ref):
+def boxcars(x, widths_ref, shifted):
     n, R, L = x.shape
     upper_tri = hot(iota((L, L), 0) < iota((L, L), 1))
     flat = x.reshape(n * R, L)
@@ -70,12 +61,20 @@
     prefix = before + run - x
     whole = jnp.sum(jnp.sum(x, axis=1, keepdims=True), axis=2, keepdims=True)
     out = jnp.zeros((n, LANES), F32)
+    rows = prefix.reshape(n * R, L)
+    for a in range(shifted.shape[0]):
+        shifted[a] = pltpu.roll(rows, L - a, 1) if a else rows
     for wi in range(widths_ref.shape[0]):
-        w = jnp.full((1, R, L), widths_ref[wi], jnp.int32)
-        y = prefix
+        width = widths_ref[wi]
+        a = lax.div(width, R)
+        w = jnp.full((1, R, L), width, jnp.int32)
+        b = w - jnp.full((1, R, L), a, jnp.int32) * R
+        here = shifted[a].reshape(n, R, L)
+        after = shifted[a + 1].reshape(n, R, L)
+        y = jnp.where(sub >= b, here, after)
         by = 1
-        while by <= WMAX:
-            y = jnp.where((w & by) != 0, shift_samples(y, by), y)
+        while by < R:
+            y = jnp.where((b & by) != 0, pltpu.roll(y, R - by, 1), y)
             by *= 2
         y = jnp.where(pos + w >= R * L, whole, y)
         top = jnp.max(jnp.max(y - prefix, axis=1), axis=1, keepdims=True)
@@ -95,6 +94,7 @@
     power,
     flag_rows,
     tops,
+    shifted,
     normed,
     perm,
     kept_all,
@@ -307,7 +307,7 @@
             series = total.reshape(PER, R, LANES)
             mean = jnp.sum(jnp.sum(series, axis=1, keepdims=True), axis=2, keepdims=True) * (1.0 / samples)
             series = series - mean
-            tops[pl.ds(pl.multiple_of(k * PER, PER), PER), :] = boxcars(series, widths_ref)
+            tops[pl.ds(pl.multiple_of(k * PER, PER), PER), :] = boxcars(series, widths_ref, shifted)
             smine[...] += jnp.sum(series * series, axis=0)
             return _
 
@@ -367,6 +367,7 @@
             pltpu.VMEM((rows, samples), F32),
             pltpu.VMEM((rfi_flags.shape[2], rows), jnp.int32),
             pltpu.VMEM((trials, LANES), F32),
+            pltpu.VMEM((WMAX // R + 2, PER * R, LANES), F32),
             pltpu.VMEM((rows, samples), F32),
             pltpu.VMEM((2 * LANES, 2 * LANES), BF16),
             pltpu.VMEM((rows, rfi_flags.shape[2]), F32),

time: 77.9 us -> 74 us (0.950)
  Pallas kernels: 75.5 us -> 71.7 us
    pallas_call x1, Pallas kernels: 75.5 us -> 71.7 us  [body(): pl.pallas_call(functools.partial(search_kernel, cfg), out_shape=(jax.Shap...]
where the time goes in v3:
time: 74 us; the launch traced here: 73.7 us
  Pallas kernels  71.7 us (97%)
  other arithmetic  2.05 us (3%)
    pallas_call x1, Pallas kernels, body(): pl.pallas_call(functools.partial(search_kernel, cfg), out_shape=(jax.Shap...  71.7 us

profile of v3, /device:TPU:0, one launch (start us, length us, event | category | flops | bytes accessed | tf_op | source)
XLA Modules:
  0.0 73.7 jit_solution(13446043464395344802)
XLA Ops:
  0.0 0.7 convert_sqrt_fusion
  0.7 71.7 %shard_map.55 = (f32[8,256]{1,0:T(8,128)}, f32[8,256]{1,0:T(8,128)}) custom-call(f32[4,512,1024]{2,1,0:T(8,128)} %spectra.1, s32[4,8,512]{2,1,0:T(8,128)} %bitcast.6, s32[64,512]{1,0:T(8,128)} %sub_delay.1, s32[64,256]{1,0:T(8,128)} %bitcast.7, s32[8]{0:T(128)} %widths_ref.1), custom_call_target="tpu_custom_call" | custom-call | tf_op jit(solution)/shard_map/pallas_call | solution.py:358
  72.3 1.4 %divide_bitcast_fusion = f32[1,256,8]{1,2,0:T(8,128)} fusion(f32[8,256]{1,0:T(8,128)} %get-tuple-element.7, f32[8,256]{1,0:T(8,128)} %get-tuple-element.8, f32[8]{0:T(128)S(1)} %convert_sqrt_fusion), kind=kLoop, calls=%fused_computation | loop fusion | flops 4096 | bytes 24608 | tf_op jit(solution)/shard_map/broadcast_in_dim | solution.py:399

commit v4 on v3

--- a/solution.py
+++ b/solution.py
@@ -334,7 +334,9 @@
     total = jnp.sum(jnp.sum(total, axis=0, keepdims=True), axis=1, keepdims=True)
     sigma = jnp.sqrt(total * (1.0 / (lanes * CD * PER * samples)) + 1e-06)
     tops_ref[...] = tops[...].T[: tops_ref.shape[0]]
-    sigma_ref[...] = jnp.broadcast_to(sigma, sigma_ref.shape)
+    for wi in range(sigma_ref.shape[0]):
+        w = jnp.full((1, sigma_ref.shape[1]), widths_ref[wi], jnp.int32).astype(F32)
+        sigma_ref[wi : wi + 1, :] = sigma * jnp.sqrt(w)
 
 
 def body(lanes, spectra, rfi_flags, sub_delay, fine_delay, widths):
@@ -395,7 +397,7 @@
             collective_id=0, has_side_effects=True, vmem_limit_bytes=60 * 1024 * 1024
         ),
     )(spectra, rfi_flags.transpose(0, 2, 1), sub_delay, fine_delay.T, widths)
-    peaks = tops / (sigma * jnp.sqrt(widths.astype(F32))[:, None])
+    peaks = tops / sigma
     return peaks.T[None]
 
 

time: 74 us -> 73.3 us (level)
  no operation moved by 1% of the time
where the time goes in v4:
time: 73.3 us; the launch traced here: 73 us
  Pallas kernels  71.7 us (98%)
  other arithmetic  1.32 us (2%)
    pallas_call x1, Pallas kernels, body(): pl.pallas_call(functools.partial(search_kernel, cfg), out_shape=(jax.Shap...  71.7 us

profile of v4, /device:TPU:0, one launch (start us, length us, event | category | flops | bytes accessed | tf_op | source)
XLA Modules:
  0.0 73.0 jit_solution(1419523094555230753)
XLA Ops:
  0.0 71.7 %shard_map.55 = (f32[8,256]{1,0:T(8,128)}, f32[8,256]{1,0:T(8,128)}) custom-call(f32[4,512,1024]{2,1,0:T(8,128)} %spectra.1, s32[4,8,512]{2,1,0:T(8,128)} %bitcast.6, s32[64,512]{1,0:T(8,128)} %sub_delay.1, s32[64,256]{1,0:T(8,128)} %bitcast.7, s32[8]{0:T(128)} %widths_ref.1), custom_call_target="tpu_custom_call" | custom-call | tf_op jit(solution)/shard_map/pallas_call | solution.py:360
  71.7 1.3 %divide_bitcast_fusion = f32[1,256,8]{1,2,0:T(8,128)} fusion(f32[8,256]{1,0:T(8,128)} %get-tuple-element.7, f32[8,256]{1,0:T(8,128)} %get-tuple-element.8), kind=kLoop, calls=%fused_computation | loop fusion | flops 2048 | bytes 24576 | tf_op jit(solution)/shard_map/broadcast_in_dim | solution.py:401
